TPU v7x, 512 devices: a whole 4x8x8 slice. The times are simulated.
512 devices in a mesh: tm: 64 (over x, y, core), dp: 8 (over z).
Axes of the slice: x: 4, y: 8, z: 8, core: 2. Of those that a mesh axis runs over, the one named last changes fastest.
Arguments:
- frame_tokens: bfloat16 [8, 192, 64, 1280], P('dp', 'tm'), may hold values from -8 to 8
- visible: int32 [8, 192, 64], P('dp'), may hold values from 0 to 2
- grad_output: bfloat16 [8, 192, 64, 1280], P('dp', 'tm'), may hold values from -16 to 16
- norm_gain: float32 [1280], replicated, may hold values from 0.1 to 1.9
- query_weight: bfloat16 [1280, 640], P('tm'), may hold values from -1.5 to 1.5
- key_weight: bfloat16 [1280, 640], P('tm'), may hold values from -1.5 to 1.5
- value_weight: bfloat16 [1280, 640], P('tm'), may hold values from -0.15625 to 0.15625
- output_weight: bfloat16 [640, 1280], P('tm'), may hold values from -0.25 to 0.25
Outputs:
- block_out: bfloat16 [8, 192, 64, 1280], P('dp', 'tm')
- grad_tokens: bfloat16 [8, 192, 64, 1280], P('dp', 'tm')
- grad_output_weight: float32 [640, 1280], P('tm')
Inputs may be any that keep to these rules, and one draw needn't show every extreme that they name: visible[c, f, g] names which of the 3 cells of group g is visible in frame f.
All inputs are finite; a program needn't handle non-finite values.
Results may differ from a plain program's by a relative error of at most 0.012.
Values may be sent and summed in bfloat16 or wider, within the bound.
No kernel may reach another device: no remote copies, remote signals or barrier semaphores. Data moves between devices by JAX's collectives and lax.ppermute only.
A program may use at most 64 MiB of HBM per device.

v0:
```python
import math

import jax
import jax.numpy as jnp
from jax import lax
from jax.sharding import PartitionSpec as P

HEADS = 8


NORM_EPS = 1e-06


def normalize(token_rows, norm_gain):
    values = token_rows.astype(jnp.float32)
    centered = values - jnp.mean(values, axis=-1, keepdims=True)
    inverse = lax.rsqrt(jnp.mean(centered * centered, axis=-1, keepdims=True) + NORM_EPS)
    scaled = centered * inverse
    return (scaled, inverse, (scaled * norm_gain).astype(jnp.bfloat16))


def project(token_rows, weight):
    lead_shape = token_rows.shape[:-1]
    flat_rows = token_rows.reshape(-1, token_rows.shape[-1])
    result = jnp.dot(flat_rows, weight, preferred_element_type=jnp.float32)
    return result.astype(jnp.bfloat16).reshape(lead_shape + (weight.shape[1],))


def split_heads(values):
    return values.reshape(values.shape[:-1] + (HEADS, values.shape[-1] // HEADS))


def attend(query_rows, key_rows, value_rows, same_cell):
    score_scale = 1.0 / math.sqrt(query_rows.shape[-1] // HEADS)
    query_heads = split_heads(query_rows)
    key_heads = split_heads(key_rows)
    value_heads = split_heads(value_rows)
    scores = (
        jnp.einsum("fghe,tghe->ghft", query_heads, key_heads, preferred_element_type=jnp.float32)
        * score_scale
    )
    scores = jnp.where(same_cell[:, None], scores, -jnp.inf)
    row_top = jnp.max(scores, axis=-1, keepdims=True)
    expons = jnp.exp(scores - row_top)
    soft_probs = expons / jnp.sum(expons, axis=-1, keepdims=True)
    probs_low = soft_probs.astype(jnp.bfloat16)
    mixed_rows = jnp.einsum(
        "ghft,tghe->fghe", probs_low, value_heads, preferred_element_type=jnp.float32
    )
    return (soft_probs, probs_low, mixed_rows.reshape(query_rows.shape).astype(jnp.bfloat16))


def attend_back(query_rows, key_rows, value_rows, soft_probs, probs_low, grad_mixed):
    score_scale = 1.0 / math.sqrt(query_rows.shape[-1] // HEADS)
    query_heads = split_heads(query_rows)
    key_heads = split_heads(key_rows)
    value_heads = split_heads(value_rows)
    grad_heads = split_heads(grad_mixed)
    grad_probs = jnp.einsum(
        "fghe,tghe->ghft", grad_heads, value_heads, preferred_element_type=jnp.float32
    )
    centre = jnp.sum(soft_probs * grad_probs, axis=-1, keepdims=True)
    grad_scores = (soft_probs * (grad_probs - centre) * score_scale).astype(jnp.bfloat16)
    grad_query = jnp.einsum(
        "ghft,tghe->fghe", grad_scores, key_heads, preferred_element_type=jnp.float32
    )
    grad_key = jnp.einsum(
        "ghft,fghe->tghe", grad_scores, query_heads, preferred_element_type=jnp.float32
    )
    grad_value = jnp.einsum(
        "ghft,fghe->tghe", probs_low, grad_heads, preferred_element_type=jnp.float32
    )
    full_shape = query_rows.shape
    return (
        grad_query.reshape(full_shape).astype(jnp.bfloat16),
        grad_key.reshape(full_shape).astype(jnp.bfloat16),
        grad_value.reshape(full_shape).astype(jnp.bfloat16),
    )


def back_project(grad_query, grad_key, grad_value, query_weight, key_weight, value_weight):
    lead_shape = grad_query.shape[:-1]
    width = grad_query.shape[-1]
    total = jnp.dot(
        grad_query.reshape(-1, width), query_weight.T, preferred_element_type=jnp.float32
    )
    total = total + jnp.dot(
        grad_key.reshape(-1, width), key_weight.T, preferred_element_type=jnp.float32
    )
    total = total + jnp.dot(
        grad_value.reshape(-1, width), value_weight.T, preferred_element_type=jnp.float32
    )
    return total.astype(jnp.bfloat16).reshape(lead_shape + (query_weight.shape[0],))


def on_device(
    frame_tokens,
    visible,
    grad_output,
    norm_gain,
    query_weight,
    key_weight,
    value_weight,
    output_weight,
):
    query_weight, key_weight, value_weight, output_weight = (
        lax.all_gather(query_weight, "tm", axis=0, tiled=True),
        lax.all_gather(key_weight, "tm", axis=0, tiled=True),
        lax.all_gather(value_weight, "tm", axis=0, tiled=True),
        lax.all_gather(output_weight, "tm", axis=0, tiled=True),
    )
    shards = lax.axis_size("tm")
    tokens = frame_tokens[0]
    frame_count, visible_count, width = tokens.shape
    att_width = output_weight.shape[0]
    groups = visible_count // shards
    scaled, inverse, normed = normalize(tokens, norm_gain)
    local_cells = lax.dynamic_slice_in_dim(visible[0], lax.axis_index("tm") * groups, groups, 1)
    cell_major = local_cells.T
    same_cell = cell_major[:, :, None] == cell_major[:, None, :]
    query_rows = project(normed, query_weight)
    key_rows = project(normed, key_weight)
    value_rows = project(normed, value_weight)
    query_rows, key_rows, value_rows = (
        lax.all_to_all(query_rows, "tm", split_axis=1, concat_axis=0, tiled=True),
        lax.all_to_all(key_rows, "tm", split_axis=1, concat_axis=0, tiled=True),
        lax.all_to_all(value_rows, "tm", split_axis=1, concat_axis=0, tiled=True),
    )
    soft_probs, probs_low, mixed_cells = attend(query_rows, key_rows, value_rows, same_cell)
    mixed_frames = lax.all_to_all(mixed_cells, "tm", split_axis=0, concat_axis=1, tiled=True)
    flat_mixed = mixed_frames.reshape(-1, att_width)
    flat_tokens = tokens.reshape(-1, width)
    update = jnp.dot(flat_mixed, output_weight, preferred_element_type=jnp.float32)
    block_rows = (
        (flat_tokens.astype(jnp.float32) + update).astype(jnp.bfloat16).reshape(tokens.shape)
    )
    flat_grad = grad_output[0].reshape(-1, width)
    grad_mixed = jnp.dot(flat_grad, output_weight.T, preferred_element_type=jnp.float32)
    grad_mixed = grad_mixed.astype(jnp.bfloat16).reshape(frame_count, visible_count, att_width)
    term_share = lax.psum_scatter(
        jnp.dot(flat_mixed.T, flat_grad, preferred_element_type=jnp.float32),
        "tm",
        scatter_dimension=0,
        tiled=True,
    )
    grad_weight = lax.psum(term_share.astype(jnp.bfloat16), "dp").astype(jnp.float32)
    grad_cells = lax.all_to_all(grad_mixed, "tm", split_axis=1, concat_axis=0, tiled=True)
    grad_query, grad_key, grad_value = attend_back(
        query_rows, key_rows, value_rows, soft_probs, probs_low, grad_cells
    )
    grad_query, grad_key, grad_value = (
        lax.all_to_all(grad_query, "tm", split_axis=0, concat_axis=1, tiled=True),
        lax.all_to_all(grad_key, "tm", split_axis=0, concat_axis=1, tiled=True),
        lax.all_to_all(grad_value, "tm", split_axis=0, concat_axis=1, tiled=True),
    )
    grad_normed = back_project(
        grad_query, grad_key, grad_value, query_weight, key_weight, value_weight
    )
    weighted = grad_normed.astype(jnp.float32) * norm_gain
    first_mean = jnp.mean(weighted, axis=-1, keepdims=True)
    second_mean = jnp.mean(weighted * scaled, axis=-1, keepdims=True)
    grad_rows = inverse * (weighted - first_mean - scaled * second_mean) + grad_output[0].astype(
        jnp.float32
    )
    return (block_rows[None], grad_rows.astype(jnp.bfloat16)[None], grad_weight)


def solution(mesh):
    return jax.shard_map(
        on_device,
        mesh=mesh,
        in_specs=(
            P("dp", "tm", None, None),
            P("dp", None, None),
            P("dp", "tm", None, None),
            P(),
            P("tm", None),
            P("tm", None),
            P("tm", None),
            P("tm", None),
        ),
        out_specs=(P("dp", "tm", None, None), P("dp", "tm", None, None), P("tm", None)),
        check_vma=False,
    )
```

profile of v0, /device:TPU:64, one launch (start us, length us, event | category | flops | bytes accessed | tf_op | source)
XLA Modules:
  0.0 840.5 jit_solution(8921300924261810447)
XLA Ops:
  12.6 85.6 %all-gather.15.cloned.1.call-done = bf16[64,10,1280]{2,1,0:T(8,128)(2,1)} async-done(((bf16[1,10,1280]{2,1,0:T(8,128)(2,1)}), bf16[64,10,1280]{2,1,0:T(8,128)(2,1)}) %all-gather.15.cloned.1.call-update) | async-done | bytes 1638416 | tf_op jit(solution)/shard_map/all_gather | solution.py:110
  98.2 2.7 reshape.316
  102.6 6.7 all-to-all-start.4
  110.7 71.2 %all-gather.13.cloned.1.call-done = bf16[64,20,640]{2,1,0:T(8,128)(2,1)} async-done(((bf16[1,20,640]{2,1,0:T(8,128)(2,1)}), bf16[64,20,640]{2,1,0:T(8,128)(2,1)}) %all-gather.13.cloned.1.call-update) | async-done | bytes 1638416 | tf_op jit(solution)/shard_map/all_gather | solution.py:108
  181.9 2.4 reshape.314
  185.9 7.0 all-to-all-start.2
  192.9 72.7 %all-gather.11.cloned.1.call-done = bf16[64,20,640]{2,1,0:T(8,128)(2,1)} async-done(((bf16[1,20,640]{2,1,0:T(8,128)(2,1)}), bf16[64,20,640]{2,1,0:T(8,128)(2,1)}) %all-gather.11.cloned.1.call-update) | async-done | bytes 1638416 | tf_op jit(solution)/shard_map/all_gather | solution.py:107
  265.7 2.4 reshape.312
  270.7 7.0 all-to-all-start.1
  277.8 71.5 %all-gather.9.cloned.1.call-done = bf16[64,20,640]{2,1,0:T(8,128)(2,1)} async-done(((bf16[1,20,640]{2,1,0:T(8,128)(2,1)}), bf16[64,20,640]{2,1,0:T(8,128)(2,1)}) %all-gather.9.cloned.1.call-update) | async-done | bytes 1638416 | tf_op jit(solution)/shard_map/all_gather | solution.py:109
  349.3 3.6 reshape.310
  352.9 2.2 convolution_convert_fusion.5
  356.0 2.2 reshape.303
  358.2 2.0 copy.53
  360.2 2.2 reshape.300
  362.4 2.0 copy.47
  364.3 7.0 all-to-all-start
  371.3 2.2 reshape.298
  373.5 2.0 copy.46
  375.5 2.9 fusion.42
  378.4 2.6 convolution_convert_fusion
  381.6 2.5 reduce.16
  387.9 10.7 %all-to-all-start.7 = ((bf16[64,2,960]{2,1,0:T(2,128)(2,1)}), bf16[64,2,960]{2,1,0:T(2,128)(2,1)}, u32[]{:S(2)}, u32[]{:S(2)}) async-start(bf16[64,2,960]{2,1,0:T(2,128)(2,1)} %reshape.328), calls=%async_computation.7 | async-start | bytes 524288 | tf_op jit(solution)/shard_map/all_to_all | solution.py:154
  398.6 2.2 reshape.296
  400.8 2.0 copy.48
  402.8 2.5 convolution_convert_fusion.1
  405.3 2.5 reduce.13
  411.6 10.5 %all-to-all-start.3 = ((bf16[64,2,960]{2,1,0:T(2,128)(2,1)}), bf16[64,2,960]{2,1,0:T(2,128)(2,1)}, u32[]{:S(2)}, u32[]{:S(2)}) async-start(bf16[64,2,960]{2,1,0:T(2,128)(2,1)} %reshape.322), calls=%async_computation.3 | async-start | bytes 524288 | tf_op jit(solution)/shard_map/all_to_all | solution.py:130
  422.1 2.6 fusion.43
  424.7 4.3 fusion.19
  429.1 2.5 reduce.15
  435.3 10.5 %all-to-all-start.6 = ((bf16[64,2,960]{2,1,0:T(2,128)(2,1)}), bf16[64,2,960]{2,1,0:T(2,128)(2,1)}, u32[]{:S(2)}, u32[]{:S(2)}) async-start(bf16[64,2,960]{2,1,0:T(2,128)(2,1)} %reshape.326), calls=%async_computation.6 | async-start | bytes 524288 | tf_op jit(solution)/shard_map/all_to_all | solution.py:153
  447.8 4.4 fusion.16
  452.1 2.5 reduce.14
  456.5 2.0 reshape.324
  458.4 2.8 reshape.329
  461.3 3.1 reduce.12
  467.8 2.8 reshape.323
  470.7 3.1 reduce.9
  477.2 10.5 %all-to-all-start.5 = ((bf16[64,2,960]{2,1,0:T(2,128)(2,1)}), bf16[64,2,960]{2,1,0:T(2,128)(2,1)}, u32[]{:S(2)}, u32[]{:S(2)}) async-start(bf16[64,2,960]{2,1,0:T(2,128)(2,1)} %reshape.324), calls=%async_computation.5 | async-start | bytes 524288 | tf_op jit(solution)/shard_map/all_to_all | solution.py:152
  487.7 2.9 reshape.327
  490.6 3.1 reduce.11
  497.1 3.0 fusion.2
  500.1 2.3 fusion.45
  502.5 2.8 reshape.325
  505.3 3.1 reduce.10
  514.9 287.3 %all-reduce.2 = bf16[640,1280]{1,0:T(8,128)(2,1)} all-reduce(f32[640,1280]{1,0:T(8,128)} %fusion.45), channel_id=2, replica_groups=mesh['tm'=64,'dp'=8] {'tm'}, use_global_device_ids=true, to_apply=%region_7.8.clone | all-reduce | flops 819200 | bytes 4915200
  803.0 29.0 %psum.7 = bf16[10,1280]{1,0:T(8,128)(2,1)S(1)} all-reduce(bf16[10,1280]{1,0:T(8,128)(2,1)S(1)} %dynamic-slice_convert_fusion), channel_id=1, replica_groups=mesh['tm'=64,'dp'=8] {'dp'}, use_global_device_ids=true, to_apply=%region_8.9 | all-reduce | flops 12800 | bytes 51200 | tf_op jit(solution)/shard_map/psum | solution.py:146
  (88 shorter events, 48.0 us)
Async XLA Ops:
  7.2 185.7 %copy-start = (s32[1,192,64]{1,2,0:T(8,128)S(1)}, s32[1,192,64]{1,2,0:T(8,128)}, u32[]{:S(2)}) copy-start(s32[1,192,64]{1,2,0:T(8,128)} %param.9) | copy-start | bytes 147460
  7.2 91.1 %all-gather.15.cloned.1.call-start = ((), (), s32[]{:S(2)}) async-start(), calls=%async_computation.11 | async-start | bytes 2662400 | tf_op jit(solution)/shard_map/all_gather | solution.py:110
  7.9 174.0 %all-gather.13.cloned.1.call-start = ((), (), s32[]{:S(2)}) async-start(), calls=%async_computation.10 | async-start | bytes 1996800 | tf_op jit(solution)/shard_map/all_gather | solution.py:108
  8.7 257.0 %all-gather.11.cloned.1.call-start = ((), (), s32[]{:S(2)}) async-start(), calls=%async_computation.9 | async-start | bytes 1996800 | tf_op jit(solution)/shard_map/all_gather | solution.py:107
  9.4 339.9 %all-gather.9.cloned.1.call-start = ((), (), s32[]{:S(2)}) async-start(), calls=%async_computation.8 | async-start | bytes 1996800 | tf_op jit(solution)/shard_map/all_gather | solution.py:109
  12.6 88.3 %copy-start.6 = (bf16[1,3,64,1280]{3,2,1,0:T(8,128)(2,1)S(1)}, bf16[1,3,64,1280]{3,2,1,0:T(8,128)(2,1)}, u32[]{:S(2)}) copy-start(bf16[1,3,64,1280]{3,2,1,0:T(8,128)(2,1)} %param.10) | copy-start | bytes 1474564
  101.0 1.7 copy-start.2
  101.0 8.4 copy-start.3
  101.0 8.4 copy-start.14
  102.6 83.2 %all-to-all-start.4 = ((bf16[3,64,640]{2,0,1:T(4,128)(2,1)}), bf16[3,64,640]{2,0,1:T(4,128)(2,1)S(1)}, u32[]{:S(2)}, u32[]{:S(2)}) async-start(bf16[3,64,640]{2,0,1:T(4,128)(2,1)} %copy.52), calls=%async_computation.4 | async-start | bytes 655360 | tf_op jit(solution)/shard_map/all_to_all | solution.py:147
  110.7 73.6 %copy-start.5 = (bf16[192,1280]{1,0:T(8,128)(2,1)}, bf16[192,1280]{1,0:T(8,128)(2,1)S(1)}, u32[]{:S(2)}) copy-start(bf16[192,1280]{1,0:T(8,128)(2,1)S(1)} %get-tuple-element.6) | copy-start | bytes 1474564
  185.9 7.1 copy-start.11
  185.9 84.8 %all-to-all-start.2 = ((bf16[3,64,640]{2,0,1:T(4,128)(2,1)}), bf16[3,64,640]{2,0,1:T(4,128)(2,1)}, u32[]{:S(2)}, u32[]{:S(2)}) async-start(bf16[3,64,640]{2,0,1:T(4,128)(2,1)} %copy.45), calls=%async_computation.2 | async-start | bytes 655360 | tf_op jit(solution)/shard_map/all_to_all | solution.py:126
  270.7 93.7 %all-to-all-start.1 = ((bf16[3,64,640]{2,0,1:T(4,128)(2,1)}), bf16[3,64,640]{2,0,1:T(4,128)(2,1)}, u32[]{:S(2)}, u32[]{:S(2)}) async-start(bf16[3,64,640]{2,0,1:T(4,128)(2,1)} %copy.44), calls=%async_computation.1 | async-start | bytes 655360 | tf_op jit(solution)/shard_map/all_to_all | solution.py:125
  364.3 23.6 %all-to-all-start = ((bf16[3,64,640]{2,0,1:T(4,128)(2,1)}), bf16[3,64,640]{2,0,1:T(4,128)(2,1)}, u32[]{:S(2)}, u32[]{:S(2)}) async-start(bf16[3,64,640]{2,0,1:T(4,128)(2,1)} %copy.43), calls=%async_computation | async-start | bytes 655360 | tf_op jit(solution)/shard_map/all_to_all | solution.py:127
  387.9 23.7 %all-to-all-start.7 = ((bf16[64,2,960]{2,1,0:T(2,128)(2,1)}), bf16[64,2,960]{2,1,0:T(2,128)(2,1)}, u32[]{:S(2)}, u32[]{:S(2)}) async-start(bf16[64,2,960]{2,1,0:T(2,128)(2,1)} %reshape.328), calls=%async_computation.7 | async-start | bytes 524288 | tf_op jit(solution)/shard_map/all_to_all | solution.py:154
  411.6 23.8 %all-to-all-start.3 = ((bf16[64,2,960]{2,1,0:T(2,128)(2,1)}), bf16[64,2,960]{2,1,0:T(2,128)(2,1)}, u32[]{:S(2)}, u32[]{:S(2)}) async-start(bf16[64,2,960]{2,1,0:T(2,128)(2,1)} %reshape.322), calls=%async_computation.3 | async-start | bytes 524288 | tf_op jit(solution)/shard_map/all_to_all | solution.py:130
  435.3 41.9 %all-to-all-start.6 = ((bf16[64,2,960]{2,1,0:T(2,128)(2,1)}), bf16[64,2,960]{2,1,0:T(2,128)(2,1)}, u32[]{:S(2)}, u32[]{:S(2)}) async-start(bf16[64,2,960]{2,1,0:T(2,128)(2,1)} %reshape.326), calls=%async_computation.6 | async-start | bytes 524288 | tf_op jit(solution)/shard_map/all_to_all | solution.py:153
  477.2 25.3 %all-to-all-start.5 = ((bf16[64,2,960]{2,1,0:T(2,128)(2,1)}), bf16[64,2,960]{2,1,0:T(2,128)(2,1)}, u32[]{:S(2)}, u32[]{:S(2)}) async-start(bf16[64,2,960]{2,1,0:T(2,128)(2,1)} %reshape.324), calls=%async_computation.5 | async-start | bytes 524288 | tf_op jit(solution)/shard_map/all_to_all | solution.py:152
  497.1 3.0 copy-start.7
  497.1 3.0 copy-start.10
  511.2 0.9 copy-start.13
  512.1 1.4 copy-start.1
  512.1 1.7 copy-start.9
  512.1 1.7 copy-start.12
  514.9 317.8 %copy-start.4 = (bf16[1,3,64,1280]{3,2,1,0:T(8,128)(2,1)S(1)}, bf16[1,3,64,1280]{3,2,1,0:T(8,128)(2,1)}, u32[]{:S(2)}) copy-start(bf16[1,3,64,1280]{3,2,1,0:T(8,128)(2,1)} %param.8) | copy-start | bytes 1474564
  514.9 317.8 %copy-start.8 = (bf16[1,3,64,1280]{3,2,1,0:T(8,128)(2,1)S(1)}, bf16[1,3,64,1280]{3,2,1,0:T(8,128)(2,1)}, u32[]{:S(2)}) copy-start(bf16[1,3,64,1280]{3,2,1,0:T(8,128)(2,1)} %param.10) | copy-start | bytes 1474564
Sparse Core Ops, SparseCore 0:
  11.3 86.8 all-gather.14
  101.5 80.3 all-gather.12
  185.2 80.4 all-gather.10
  268.8 80.4 all-gather.8
where the time goes:
time: 843 us; the launch traced here: 840 us
  blocking collectives  316 us (37%)
  waiting for transfers between devices  304 us (36%)
  local copies, waits for them, and re-layouts  75.6 us (9%)
  starting transfers between devices  70.1 us (8%)
  matrix products  31.9 us (4%)
  other arithmetic  28.2 us (3%)
  between operations  14.7 us (2%)
    unnamed x1, blocking collectives  287 us
    all_gather x1, waiting for transfers between devices, on_device(): lax.all_gather(output_weight, 'tm', axis=0, tiled=True)  85.6 us
    all_gather x1, waiting for transfers between devices, on_device(): lax.all_gather(query_weight, 'tm', axis=0, tiled=True)  72.7 us
    all_gather x1, waiting for transfers between devices, on_device(): lax.all_gather(value_weight, 'tm', axis=0, tiled=True)  71.5 us
    all_gather x1, waiting for transfers between devices, on_device(): lax.all_gather(key_weight, 'tm', axis=0, tiled=True)  71.2 us
    unnamed x47, local copies, waits for them, and re-layouts  40.3 us
    psum x1, blocking collectives, on_device(): lax.psum(term_share.astype(jnp.bfloat16), 'dp').astype(jnp.float32)  29 us
  transfers between devices with their start and end apart: 12, of which 4 were waited for; matrix products, arithmetic and copies ran while one was open for 14% of the time, Pallas kernels for 0%

commit v1 on v0

v1 whole, which is shorter than its diff:
```python
import functools
import math

import jax
import jax.numpy as jnp
from jax import lax
from jax.experimental import pallas as pl
from jax.experimental.pallas import tpu as pltpu
from jax.sharding import Mesh
from jax.sharding import PartitionSpec as P

HEADS = 8
NORM_EPS = 1e-06
PARTS = ("x", "y", "core")
SIZES = (4, 8, 2)


def dot(left, right, contract):
    return lax.dot_general(
        left, right, (contract, ((), ())), preferred_element_type=jnp.float32
    )


NN = ((1,), (0,))
NT = ((1,), (1,))
TN = ((0,), (0,))


def cell_kernel(normed_ref, grad_ref, row_ref, col_ref, qkv_ref, out_ref,
                mixed_ref, normed_grad_ref, weight_ref):
    low = jnp.bfloat16
    att = out_ref.shape[0]
    size = att // HEADS
    scale = 1.0 / math.sqrt(size)
    qkv = dot(normed_ref[...], qkv_ref[...], NN).astype(low)
    grad_mixed = dot(grad_ref[...], out_ref[...], NT).astype(low)
    same = row_ref[...] == col_ref[...]
    mixed, grad_q, grad_k, grad_v = [], [], [], []
    for h in range(HEADS):
        q = qkv[:, h * size:(h + 1) * size]
        k = qkv[:, att + h * size:att + (h + 1) * size]
        v = qkv[:, 2 * att + h * size:2 * att + (h + 1) * size]
        g = grad_mixed[:, h * size:(h + 1) * size]
        scores = jnp.where(same, dot(q, k, NT) * scale, -jnp.inf)
        expons = jnp.exp(scores - jnp.max(scores, axis=-1, keepdims=True))
        probs = expons / jnp.sum(expons, axis=-1, keepdims=True)
        probs_low = probs.astype(low)
        mixed.append(dot(probs_low, v, NN).astype(low))
        grad_probs = dot(g, v, NT)
        centre = jnp.sum(probs * grad_probs, axis=-1, keepdims=True)
        grad_scores = (probs * (grad_probs - centre) * scale).astype(low)
        grad_q.append(dot(grad_scores, k, NN).astype(low))
        grad_k.append(dot(grad_scores, q, TN).astype(low))
        grad_v.append(dot(probs_low, g, TN).astype(low))
    mixed = jnp.concatenate(mixed, axis=1)
    mixed_ref[...] = mixed
    grads = jnp.concatenate(grad_q + grad_k + grad_v, axis=1)
    normed_grad_ref[...] = dot(grads, qkv_ref[...], NT).astype(low)
    weight_ref[...] = dot(mixed, grad_ref[...], TN).astype(low)


def cell_part(normed, grad, cells, qkv_weight, output_weight, interpret=False):
    rows, width = normed.shape
    att = output_weight.shape[0]
    low = jnp.bfloat16
    return pl.pallas_call(
        cell_kernel,
        out_shape=(
            jax.ShapeDtypeStruct((rows, att), low),
            jax.ShapeDtypeStruct((rows, width), low),
            jax.ShapeDtypeStruct((att, width), low),
        ),
        compiler_params=pltpu.CompilerParams(vmem_limit_bytes=48 << 20),
        interpret=interpret,
    )(normed, grad, cells[:, None], cells[None, :], qkv_weight, output_weight)


def exchange(values, axis):
    return lax.all_to_all(values, axis, split_axis=0, concat_axis=0, tiled=True)


def add_up(parts):
    return jnp.sum(parts.astype(jnp.float32), axis=0)


def on_device(frame_tokens, visible, grad_output, norm_gain,
              query_weight, key_weight, value_weight, output_weight):
    low = jnp.bfloat16
    shards = SIZES[0] * SIZES[1] * SIZES[2]
    tokens = frame_tokens[0]
    frames, groups, width = tokens.shape
    att = query_weight.shape[1]
    depth = query_weight.shape[0]
    me = lax.axis_index(PARTS)

    share = jnp.concatenate(
        [query_weight, key_weight, value_weight, output_weight.reshape(depth, att)], axis=1
    )
    whole = lax.all_gather(share, PARTS, axis=0, tiled=False)
    qkv_weight = whole[:, :, :3 * att].reshape(width, 3 * att)
    whole_out = whole[:, :, 3 * att:].reshape(att, width)

    values = tokens.astype(jnp.float32)
    centered = values - jnp.mean(values, axis=-1, keepdims=True)
    inverse = lax.rsqrt(jnp.mean(centered * centered, axis=-1, keepdims=True) + NORM_EPS)
    scaled = centered * inverse
    normed = (scaled * norm_gain).astype(low)

    def to_cells(rows):
        sent = rows.transpose(1, 0, 2).reshape(shards, 2, -1)
        return exchange(sent, PARTS).reshape(shards * frames, -1)

    def to_frames(rows):
        sent = rows.reshape(shards, 2, -1)
        return exchange(sent, PARTS).reshape(shards, frames, -1).transpose(1, 0, 2)

    normed_cells = to_cells(normed)
    grad_cells = to_cells(grad_output[0])
    cells = lax.dynamic_slice_in_dim(visible[0], me, 1, 1)[:, 0]
    mixed_cells, grad_normed_cells, weight_part = cell_part(
        normed_cells, grad_cells, cells, qkv_weight, whole_out
    )
    mixed = to_frames(mixed_cells)
    grad_normed = to_frames(grad_normed_cells)

    halves = weight_part.reshape(att, 2, width // 2).transpose(1, 0, 2)
    part = add_up(exchange(halves, "core")).astype(low)
    part = add_up(exchange(part.reshape(SIZES[0], -1, width // 2), "x")).astype(low)
    part = add_up(exchange(part.reshape(SIZES[1], -1, width // 2), "y")).astype(low)
    part = add_up(exchange(jnp.broadcast_to(part[None], (8,) + part.shape), "dp"))
    part = exchange(part.reshape(2, -1, width // 2), "core")
    grad_weight = part.transpose(1, 0, 2).reshape(-1, width)

    flat_mixed = mixed.reshape(-1, att)
    update = jnp.dot(flat_mixed, whole_out, preferred_element_type=jnp.float32)
    block_rows = (values.reshape(-1, width) + update).astype(low).reshape(tokens.shape)
    weighted = grad_normed.astype(jnp.float32) * norm_gain
    first_mean = jnp.mean(weighted, axis=-1, keepdims=True)
    second_mean = jnp.mean(weighted * scaled, axis=-1, keepdims=True)
    grad_rows = inverse * (weighted - first_mean - scaled * second_mean)
    grad_rows = grad_rows + grad_output[0].astype(jnp.float32)
    return (block_rows[None], grad_rows.astype(low)[None], grad_weight)


def solution(mesh):
    fine = Mesh(mesh.devices.reshape(SIZES + (mesh.shape["dp"],)), PARTS + ("dp",))
    rows = P("dp", PARTS, None, None)
    weight = P(PARTS, None)
    return jax.shard_map(
        on_device,
        mesh=fine,
        in_specs=(rows, P("dp", None, None), rows, P(), weight, weight, weight, weight),
        out_specs=(rows, rows, weight),
        check_vma=False,
    )
```

time: 843 us -> 250 us (0.30)
  the two profiles are of different devices: /device:TPU:64 before, /device:TPU:7 now
where the time goes in v1:
time: 250 us; the launch traced here: 249 us
  waiting for transfers between devices  113 us (45%)
  starting transfers between devices  48.9 us (20%)
  local copies, waits for them, and re-layouts  37.7 us (15%)
  between operations  14.3 us (6%)
  blocking collectives  11.2 us (4%)
  other arithmetic  10.8 us (4%)
  Pallas kernels  10.4 us (4%)
  matrix products  2.54 us (1%)
    all_to_all x7, waiting for transfers between devices, exchange(): return lax.all_to_all(values, axis, split_axis=0, concat_axis=0, tiled=True)  75.6 us
    all_to_all x7, starting transfers between devices, exchange(): return lax.all_to_all(values, axis, split_axis=0, concat_axis=0, tiled=True)  48.8 us
    all_gather x1, waiting for transfers between devices, on_device(): whole = lax.all_gather(share, PARTS, axis=0, tiled=False)  37.6 us
    all_to_all x2, blocking collectives, exchange(): return lax.all_to_all(values, axis, split_axis=0, concat_axis=0, tiled=True)  11.2 us
    pallas_call x1, Pallas kernels, cell_part(): pl.pallas_call(cell_kernel, out_shape=(jax.ShapeDtypeStruct((rows, att),...  10.4 us
    reshape x1, local copies, waits for them, and re-layouts, on_device(): qkv_weight = whole[:, :, :3 * att].reshape(width, 3 * att)  7.52 us
    slice x1, local copies, waits for them, and re-layouts, on_device(): qkv_weight = whole[:, :, :3 * att].reshape(width, 3 * att)  5.7 us
  transfers between devices with their start and end apart: 8, of which 8 were waited for; matrix products, arithmetic and copies ran while one was open for 9% of the time, Pallas kernels for 0%

profile of v1, /device:TPU:7, one launch (start us, length us, event | category | flops | bytes accessed | tf_op | source)
XLA Modules:
  0.0 249.0 jit_solution(11101847600365802203)
XLA Ops:
  7.2 0.8 reshape.90
  8.1 1.5 maximum_bitcast_fusion
  9.6 1.5 convert_reduce_fusion
  11.0 0.6 multiply_reduce_fusion
  11.7 0.6 fusion.7
  12.3 1.3 reshape.86
  13.7 11.1 %all-to-all-start = ((bf16[64,2,1920]{2,1,0:T(2,128)(2,1)}), bf16[64,2,1920]{2,1,0:T(2,128)(2,1)S(1)}, u32[]{:S(2)}, u32[]{:S(2)}) async-start(bf16[64,2,1920]{2,1,0:T(2,128)(2,1)} %reshape.86), calls=%async_computation | async-start | bytes 983040 | tf_op jit(solution)/shard_map/all_to_all | solution.py:79
  24.8 0.4 copy.71
  25.2 1.3 reshape.88
  26.6 15.9 %all-to-all-done = bf16[64,2,1920]{2,1,0:T(2,128)(2,1)S(1)} async-done(((bf16[64,2,1920]{2,1,0:T(2,128)(2,1)}), bf16[64,2,1920]{2,1,0:T(2,128)(2,1)S(1)}, u32[]{:S(2)}, u32[]{:S(2)}) %all-to-all-start) | async-done | bytes 491552 | tf_op jit(solution)/shard_map/all_to_all | solution.py:79
  42.5 6.5 %all-to-all-start.1 = ((bf16[64,2,1920]{2,1,0:T(2,128)(2,1)}), bf16[64,2,1920]{2,1,0:T(2,128)(2,1)S(1)}, u32[]{:S(2)}, u32[]{:S(2)}) async-start(bf16[64,2,1920]{2,1,0:T(2,128)(2,1)} %reshape.88), calls=%async_computation.1 | async-start | bytes 983040 | tf_op jit(solution)/shard_map/all_to_all | solution.py:79
  49.0 0.7 dynamic-slice_bitcast_fusion
  50.1 15.3 %all-to-all-done.1 = bf16[64,2,1920]{2,1,0:T(2,128)(2,1)S(1)} async-done(((bf16[64,2,1920]{2,1,0:T(2,128)(2,1)}), bf16[64,2,1920]{2,1,0:T(2,128)(2,1)S(1)}, u32[]{:S(2)}, u32[]{:S(2)}) %all-to-all-start.1) | async-done | bytes 491552 | tf_op jit(solution)/shard_map/all_to_all | solution.py:79
  65.8 37.6 %all-gather.4.cloned.1.call-done = bf16[64,20,2560]{2,1,0:T(8,128)(2,1)} async-done(((bf16[1,20,2560]{2,1,0:T(8,128)(2,1)}), bf16[64,20,2560]{2,1,0:T(8,128)(2,1)}) %all-gather.4.cloned.1.call-update) | async-done | bytes 6553616 | tf_op jit(solution)/shard_map/all_gather | solution.py:99
  103.4 3.1 %slice.9 = bf16[64,20,640]{2,1,0:T(8,128)(2,1)} slice(bf16[64,20,2560]{2,1,0:T(8,128)(2,1)} %all-gather.4.cloned.1.call-done), slice={[0:64], [0:20], [1920:2560]} | slice | bytes 3276800 | tf_op jit(solution)/shard_map/slice | solution.py:101
  106.5 2.7 %reshape.92.out_ref = bf16[640,1280]{1,0:T(8,128)(2,1)S(1)} reshape(bf16[64,20,640]{2,1,0:T(8,128)(2,1)} %slice.9) | data formatting | bytes 3276800 | tf_op jit(solution)/shard_map/reshape | solution.py:101
  109.2 5.7 %slice.8 = bf16[64,20,1920]{2,1,0:T(8,128)(2,1)} slice(bf16[64,20,2560]{2,1,0:T(8,128)(2,1)} %all-gather.4.cloned.1.call-done), slice={[0:64], [0:20], [0:1920]} | slice | bytes 9830400 | tf_op jit(solution)/shard_map/slice | solution.py:100
  114.9 7.5 %reshape.91.qkv_ref = bf16[1280,1920]{1,0:T(8,128)(2,1)} reshape(bf16[64,20,1920]{2,1,0:T(8,128)(2,1)} %slice.8) | data formatting | bytes 9830400 | tf_op jit(solution)/shard_map/reshape | solution.py:100
  122.4 10.4 %shard_map.103 = (bf16[192,640]{1,0:T(8,128)(2,1)S(1)}, bf16[192,1280]{1,0:T(8,128)(2,1)S(1)}, bf16[640,1280]{1,0:T(8,128)(2,1)S(1)}) custom-call(bf16[192,1280]{1,0:T(8,128)(2,1)S(1)} %reshape.87.normed_ref, bf16[192,1280]{1,0:T(8,128)(2,1)S(1)} %reshape.89.grad_ref, s32[192,1]{1,0:T(8,128)S(1)} %copy.52.row_ref, s32[1,192]{1,0:T(1,128)S(1)} %get-tuple-element.29.col_ref, ...), custom_call_target="tpu_custom_call" | custom-call | tf_op jit(solution)/shard_map/pallas_call | solution.py:66
  132.9 1.2 copy-done
  134.0 1.0 reshape.93
  135.1 1.6 copy.70
  136.6 5.8 %all_to_all.45 = bf16[2,640,640]{2,1,0:T(8,128)(2,1)} all-to-all(bf16[2,640,640]{2,1,0:T(8,128)(2,1)S(1)} %bitcast.69), channel_id=1, replica_groups=mesh['x'=4,'y'=8,'core'=2,'dp'=8] {'core'}, dimensions={0} | all-to-all | bytes 3276800 | tf_op jit(solution)/shard_map/all_to_all | solution.py:79
  142.4 8.2 %all-to-all-start.2 = ((bf16[64,2,960]{2,1,0:T(2,128)(2,1)}), bf16[64,2,960]{2,1,0:T(2,128)(2,1)S(1)}, u32[]{:S(2)}, u32[]{:S(2)}) async-start(bf16[64,2,960]{2,1,0:T(2,128)(2,1)} %reshape.93), calls=%async_computation.2 | async-start | bytes 524288 | tf_op jit(solution)/shard_map/all_to_all | solution.py:79
  150.7 2.8 %reduce_sum.85 = bf16[640,640]{1,0:T(8,128)(2,1)} reduce(bf16[2,640,640]{2,1,0:T(8,128)(2,1)} %all_to_all.45, bf16[]{:T(256)} %constant.37.clone.1), dimensions={0}, to_apply=%region_4.0 | reduce | flops 409600 | bytes 2457602 | tf_op jit(solution)/shard_map/reduce_sum | solution.py:83
  153.5 8.7 %all-to-all-done.2 = bf16[64,2,960]{2,1,0:T(2,128)(2,1)S(1)} async-done(((bf16[64,2,960]{2,1,0:T(2,128)(2,1)}), bf16[64,2,960]{2,1,0:T(2,128)(2,1)S(1)}, u32[]{:S(2)}, u32[]{:S(2)}) %all-to-all-start.2) | async-done | bytes 245792 | tf_op jit(solution)/shard_map/all_to_all | solution.py:79
  162.2 0.7 copy-done.5
  162.9 4.1 %all-to-all-start.5 = ((bf16[4,160,640]{2,1,0:T(8,128)(2,1)}), bf16[4,160,640]{2,1,0:T(8,128)(2,1)S(1)}, u32[]{:S(2)}, u32[]{:S(2)}) async-start(bf16[4,160,640]{2,1,0:T(8,128)(2,1)} %bitcast.71), calls=%async_computation.5 | async-start | bytes 1638400 | tf_op jit(solution)/shard_map/all_to_all | solution.py:79
  167.1 1.1 reshape.96
  168.1 9.2 %all-to-all-done.5 = bf16[4,160,640]{2,1,0:T(8,128)(2,1)S(1)} async-done(((bf16[4,160,640]{2,1,0:T(8,128)(2,1)}), bf16[4,160,640]{2,1,0:T(8,128)(2,1)S(1)}, u32[]{:S(2)}, u32[]{:S(2)}) %all-to-all-start.5) | async-done | bytes 819232 | tf_op jit(solution)/shard_map/all_to_all | solution.py:79
  177.3 8.4 %all-to-all-start.3 = ((bf16[64,2,1920]{2,1,0:T(2,128)(2,1)}), bf16[64,2,1920]{2,1,0:T(2,128)(2,1)S(1)}, u32[]{:S(2)}, u32[]{:S(2)}) async-start(bf16[64,2,1920]{2,1,0:T(2,128)(2,1)} %reshape.96), calls=%async_computation.3 | async-start | bytes 983040 | tf_op jit(solution)/shard_map/all_to_all | solution.py:79
  186.2 1.1 copy.50
  187.3 2.0 reshape.94
  189.4 1.0 copy.53
  190.4 2.5 %fusion = bf16[192,1280]{1,0:T(8,128)(2,1)} fusion(f32[192,1280]{1,0:T(8,128)} %bitcast.70, bf16[192,640]{1,0:T(8,128)(2,1)S(1)} %bitcast.74, bf16[640,1280]{1,0:T(8,128)(2,1)S(1)} %reshape.92.out_ref), kind=kOutput, calls=%fused_computation.1 | convolution fusion | flops 315064320 | bytes 3358720 | tf_op jit(solution)/shard_map/dot_general | solution.py:135
  193.0 0.7 reshape.99
  193.8 8.4 %all-to-all-done.3 = bf16[64,2,1920]{2,1,0:T(2,128)(2,1)S(1)} async-done(((bf16[64,2,1920]{2,1,0:T(2,128)(2,1)}), bf16[64,2,1920]{2,1,0:T(2,128)(2,1)S(1)}, u32[]{:S(2)}, u32[]{:S(2)}) %all-to-all-start.3) | async-done | bytes 491552 | tf_op jit(solution)/shard_map/all_to_all | solution.py:79
  202.2 3.4 %all-to-all-start.6 = ((bf16[8,20,640]{2,1,0:T(8,128)(2,1)}), bf16[8,20,640]{2,1,0:T(8,128)(2,1)S(1)}, u32[]{:S(2)}, u32[]{:S(2)}) async-start(bf16[8,20,640]{2,1,0:T(8,128)(2,1)} %reshape.99), calls=%async_computation.6 | async-start | bytes 491520 | tf_op jit(solution)/shard_map/all_to_all | solution.py:79
  205.6 0.5 reshape.103
  206.1 1.0 bitcast_reduce_fusion
  207.2 10.4 %all-to-all-done.6 = bf16[8,20,640]{2,1,0:T(8,128)(2,1)S(1)} async-done(((bf16[8,20,640]{2,1,0:T(8,128)(2,1)}), bf16[8,20,640]{2,1,0:T(8,128)(2,1)S(1)}, u32[]{:S(2)}, u32[]{:S(2)}) %all-to-all-start.6) | async-done | bytes 204832 | tf_op jit(solution)/shard_map/all_to_all | solution.py:79
  217.6 0.7 broadcast_in_dim.5
  218.3 7.1 %all-to-all-start.7 = ((bf16[8,20,640]{2,1,0:T(8,128)(2,1)}), bf16[8,20,640]{2,1,0:T(8,128)(2,1)S(1)}, u32[]{:S(2)}, u32[]{:S(2)}) async-start(bf16[8,20,640]{2,1,0:T(8,128)(2,1)} %broadcast_in_dim.5), calls=%async_computation.7 | async-start | bytes 491520 | tf_op jit(solution)/shard_map/all_to_all | solution.py:79
  225.4 2.0 fusion.8
  227.5 0.8 copy.57
  228.3 7.6 %all-to-all-done.7 = bf16[8,20,640]{2,1,0:T(8,128)(2,1)S(1)} async-done(((bf16[8,20,640]{2,1,0:T(8,128)(2,1)}), bf16[8,20,640]{2,1,0:T(8,128)(2,1)S(1)}, u32[]{:S(2)}, u32[]{:S(2)}) %all-to-all-start.7) | async-done | bytes 204832 | tf_op jit(solution)/shard_map/all_to_all | solution.py:79
  236.0 5.4 %all_to_all.46 = f32[2,10,640]{2,1,0:T(8,128)S(1)} all-to-all(f32[2,10,640]{2,1,0:T(8,128)S(1)} %reshape.100), channel_id=1, replica_groups=mesh['x'=4,'y'=8,'core'=2,'dp'=8] {'core'}, dimensions={0} | all-to-all | bytes 102400 | tf_op jit(solution)/shard_map/all_to_all | solution.py:79
  241.5 0.6 copy.59
  (27 shorter events, 1.6 us)
Async XLA Ops:
  7.2 3.9 %copy-start.1 = (bf16[1,3,64,1280]{3,2,1,0:T(8,128)(2,1)S(1)}, bf16[1,3,64,1280]{3,2,1,0:T(8,128)(2,1)}, u32[]{:S(2)}) copy-start(bf16[1,3,64,1280]{3,2,1,0:T(8,128)(2,1)} %param.8) | copy-start | bytes 1474564
  7.2 4.5 %copy-start.6 = (f32[1280]{0:T(1024)S(1)}, f32[1280]{0:T(1024)}, u32[]{:S(2)}) copy-start(f32[1280]{0:T(1024)} %param.11) | copy-start | bytes 15364
  7.2 96.2 %all-gather.4.cloned.1.call-start = ((), (), s32[]{:S(2)}) async-start(), calls=%async_computation.9 | async-start | bytes 7987200 | tf_op jit(solution)/shard_map/all_gather | solution.py:99
  12.3 12.5 %copy-start.3 = (bf16[1,3,64,1280]{3,2,1,0:T(8,128)(2,1)S(1)}, bf16[1,3,64,1280]{3,2,1,0:T(8,128)(2,1)}, u32[]{:S(2)}) copy-start(bf16[1,3,64,1280]{3,2,1,0:T(8,128)(2,1)} %param.10) | copy-start | bytes 1474564
  13.7 28.8 %all-to-all-start = ((bf16[64,2,1920]{2,1,0:T(2,128)(2,1)}), bf16[64,2,1920]{2,1,0:T(2,128)(2,1)S(1)}, u32[]{:S(2)}, u32[]{:S(2)}) async-start(bf16[64,2,1920]{2,1,0:T(2,128)(2,1)} %reshape.86), calls=%async_computation | async-start | bytes 983040 | tf_op jit(solution)/shard_map/all_to_all | solution.py:79
  42.5 23.0 %all-to-all-start.1 = ((bf16[64,2,1920]{2,1,0:T(2,128)(2,1)}), bf16[64,2,1920]{2,1,0:T(2,128)(2,1)S(1)}, u32[]{:S(2)}, u32[]{:S(2)}) async-start(bf16[64,2,1920]{2,1,0:T(2,128)(2,1)} %reshape.88), calls=%async_computation.1 | async-start | bytes 983040 | tf_op jit(solution)/shard_map/all_to_all | solution.py:79
  132.9 1.2 copy-start
  142.4 19.8 %all-to-all-start.2 = ((bf16[64,2,960]{2,1,0:T(2,128)(2,1)}), bf16[64,2,960]{2,1,0:T(2,128)(2,1)S(1)}, u32[]{:S(2)}, u32[]{:S(2)}) async-start(bf16[64,2,960]{2,1,0:T(2,128)(2,1)} %reshape.93), calls=%async_computation.2 | async-start | bytes 524288 | tf_op jit(solution)/shard_map/all_to_all | solution.py:79
  162.2 0.7 copy-start.5
  162.9 14.4 %all-to-all-start.5 = ((bf16[4,160,640]{2,1,0:T(8,128)(2,1)}), bf16[4,160,640]{2,1,0:T(8,128)(2,1)S(1)}, u32[]{:S(2)}, u32[]{:S(2)}) async-start(bf16[4,160,640]{2,1,0:T(8,128)(2,1)} %bitcast.71), calls=%async_computation.5 | async-start | bytes 1638400 | tf_op jit(solution)/shard_map/all_to_all | solution.py:79
  167.1 18.7 %copy-start.2 = (bf16[1,3,64,1280]{3,2,1,0:T(8,128)(2,1)S(1)}, bf16[1,3,64,1280]{3,2,1,0:T(8,128)(2,1)}, u32[]{:S(2)}) copy-start(bf16[1,3,64,1280]{3,2,1,0:T(8,128)(2,1)} %param.8) | copy-start | bytes 1474564
  177.3 24.9 %all-to-all-start.3 = ((bf16[64,2,1920]{2,1,0:T(2,128)(2,1)}), bf16[64,2,1920]{2,1,0:T(2,128)(2,1)S(1)}, u32[]{:S(2)}, u32[]{:S(2)}) async-start(bf16[64,2,1920]{2,1,0:T(2,128)(2,1)} %reshape.96), calls=%async_computation.3 | async-start | bytes 983040 | tf_op jit(solution)/shard_map/all_to_all | solution.py:79
  202.2 15.4 %all-to-all-start.6 = ((bf16[8,20,640]{2,1,0:T(8,128)(2,1)}), bf16[8,20,640]{2,1,0:T(8,128)(2,1)S(1)}, u32[]{:S(2)}, u32[]{:S(2)}) async-start(bf16[8,20,640]{2,1,0:T(8,128)(2,1)} %reshape.99), calls=%async_computation.6 | async-start | bytes 491520 | tf_op jit(solution)/shard_map/all_to_all | solution.py:79
  206.1 19.3 %copy-start.4 = (bf16[1,3,64,1280]{3,2,1,0:T(8,128)(2,1)S(1)}, bf16[1,3,64,1280]{3,2,1,0:T(8,128)(2,1)}, u32[]{:S(2)}) copy-start(bf16[1,3,64,1280]{3,2,1,0:T(8,128)(2,1)} %param.10) | copy-start | bytes 1474564
  218.3 17.6 %all-to-all-start.7 = ((bf16[8,20,640]{2,1,0:T(8,128)(2,1)}), bf16[8,20,640]{2,1,0:T(8,128)(2,1)S(1)}, u32[]{:S(2)}, u32[]{:S(2)}) async-start(bf16[8,20,640]{2,1,0:T(8,128)(2,1)} %broadcast_in_dim.5), calls=%async_computation.7 | async-start | bytes 491520 | tf_op jit(solution)/shard_map/all_to_all | solution.py:79
Sparse Core Ops, SparseCore 0:
  11.3 92.0 all-gather.3
